TPU v7x, 32 devices: a whole 2x2x4 slice. The times are simulated.
32 devices in a mesh: dp: 4 (over y, x), row: 4 (over z), col: 2 (over core).
Axes of the slice: x: 2, y: 2, z: 4, core: 2. Of those that a mesh axis runs over, the one named last changes fastest.
Arguments:
- images: bfloat16 [32, 577, 1024], P(('dp', 'row'), None, 'col'), may hold values from -6 to 6
- cotangent: bfloat16 [32, 577, 1024], P(('dp', 'row'), None, 'col'), may hold values from -6 to 6
- micro_batch: int32 [32], P(('dp', 'row')), may hold values from 0 to 1, as said below
- heads_weight: bfloat16 [1024, 3, 1024], P('row', None, 'col'), may hold values from -0.1875 to 0.1875
- heads_bias: bfloat16 [2, 1024], P(None, 'col'), may hold values from -3 to 3
- merge_weight: bfloat16 [1024, 1024], P('col', 'row'), may hold values from -2 to 2
- merge_bias: bfloat16 [1024], P('col'), may hold values from -3 to 3
- expand_weight: bfloat16 [1024, 4096], P('row', 'col'), may hold values from -0.1875 to 0.1875
- expand_bias: bfloat16 [4096], P('col'), may hold values from -3 to 3
- shrink_weight: bfloat16 [4096, 1024], P('col', 'row'), may hold values from -0.09375 to 0.09375
- shrink_bias: bfloat16 [1024], P('col'), may hold values from -3 to 3
- norm_gains: bfloat16 [2, 1024], P(None, 'col'), may hold values from 0.5 to 1.5
- norm_shifts: bfloat16 [2, 1024], P(None, 'col'), may hold values from -2 to 2
Outputs:
- block_out: bfloat16 [32, 577, 1024], P(('dp', 'row'), None, 'col')
- input_grad: float32 [32, 577, 1024], P(('dp', 'row'), None, 'col')
- heads_weight_grad: float32 [1024, 3, 1024], P('row', None, 'col')
- heads_bias_grad: float32 [2, 1024], P(None, 'col')
- merge_weight_grad: float32 [1024, 1024], P('col', 'row')
- merge_bias_grad: float32 [1024], P('col')
- expand_weight_grad: float32 [1024, 4096], P('row', 'col')
- expand_bias_grad: float32 [4096], P('col')
- shrink_weight_grad: float32 [4096, 1024], P('col', 'row')
- shrink_bias_grad: float32 [1024], P('col')
- norm_gains_grad: float32 [2, 1024], P(None, 'col')
- norm_shifts_grad: float32 [2, 1024], P(None, 'col')
Inputs may be any that keep to these rules, and one draw needn't show every extreme that they name: `micro_batch`: every micro-batch number 0 to 1 belongs to at least one image.
All inputs are finite; a program needn't handle non-finite values.
Results may differ from a plain program's by a relative error of at most 0.018.
Values may be sent and summed in bfloat16 or wider, within the bound.
No kernel may reach another device: no remote copies, remote signals or barrier semaphores. Data moves between devices by JAX's collectives and lax.ppermute only.
A program may use at most 192 MiB of HBM per device.

v0:
```python
import jax
import jax.numpy as jnp
from jax import lax
from jax.sharding import PartitionSpec as P

HEAD_DIM = 64
MICRO = 2


def merged(value, axis, join):
    pieces = jax.tree.map(lambda part: lax.all_gather(part, axis), value)
    head = jax.tree.map(lambda part: part[0], pieces)
    tail = jax.tree.map(lambda part: part[1:], pieces)
    subtotal, _ = lax.scan(lambda subtotal, share: (join(subtotal, share), None), head, tail)
    return subtotal


def moments_join(first, second):
    count_sum = first[0] + second[0]
    offset = second[1] - first[1]
    joined_mean = first[1] + offset * (second[0] / count_sum)
    joined_spread = first[2] + second[2] + offset * offset * (first[0] * second[0] / count_sum)
    return (count_sum, joined_mean, joined_spread)


def norm_split(values, gain, shift, full_width):
    local_mean = jnp.mean(values, axis=1)
    local_spread = jnp.sum(jnp.square(values - local_mean[:, None]), axis=1)
    local_count = jnp.full(local_mean.shape, values.shape[1], jnp.float32)
    merged_count, row_mean, row_spread = merged(
        (local_count, local_mean, local_spread), "col", moments_join
    )
    inverse = lax.rsqrt(row_spread / full_width + 1e-05)
    centered = (values - row_mean[:, None]) * inverse[:, None]
    normed = (centered * gain + shift).astype(jnp.bfloat16)
    return (lax.all_gather(normed, "col", axis=1, tiled=True), centered, inverse)


def norm_back_split(partial_rows, centered, inverse, gain, full_width):
    summed = lax.psum_scatter(
        partial_rows.astype(jnp.bfloat16), "col", scatter_dimension=1, tiled=True
    ).astype(jnp.float32)
    scaled = summed * gain
    first_total, second_total = lax.psum(
        (jnp.sum(scaled, axis=1), jnp.sum(scaled * centered, axis=1)), "col"
    )
    result = inverse[:, None] * (
        scaled - first_total[:, None] / full_width - centered * (second_total[:, None] / full_width)
    )
    return (result, jnp.sum(summed * centered, axis=0), jnp.sum(summed, axis=0))


def gather_grads(values):
    return lax.all_gather(values, "col", axis=1, tiled=True)


def branch_split(partial_rows):
    return lax.psum_scatter(
        partial_rows.astype(jnp.bfloat16), "col", scatter_dimension=1, tiled=True
    ).astype(jnp.float32)


def attend(query_low, key_low, value_low):
    scores = jnp.einsum("qhe,khe->hqk", query_low, key_low, preferred_element_type=jnp.float32)
    log_total = jax.nn.logsumexp(scores, axis=-1)
    probabilities = jnp.exp(scores - log_total[..., None]).astype(jnp.bfloat16)
    attended = jnp.einsum(
        "hqk,khe->qhe", probabilities, value_low, preferred_element_type=jnp.float32
    )
    return (attended, log_total)


def attend_back(query_low, key_low, value_low, log_total, upstream):
    scores = jnp.einsum("qhe,khe->hqk", query_low, key_low, preferred_element_type=jnp.float32)
    probabilities = jnp.exp(scores - log_total[..., None])
    probs_low = probabilities.astype(jnp.bfloat16)
    value_grad = jnp.einsum(
        "hqk,qhe->khe", probs_low, upstream, preferred_element_type=jnp.float32
    ).astype(jnp.bfloat16)
    prob_grad = jnp.einsum("qhe,khe->hqk", upstream, value_low, preferred_element_type=jnp.float32)
    score_grad = (
        probabilities * (prob_grad - jnp.sum(prob_grad * probabilities, axis=-1, keepdims=True))
    ).astype(jnp.bfloat16)
    query_grad = jnp.einsum(
        "hqk,khe->qhe", score_grad, key_low, preferred_element_type=jnp.float32
    ).astype(jnp.bfloat16)
    key_grad = jnp.einsum(
        "hqk,qhe->khe", score_grad, query_low, preferred_element_type=jnp.float32
    ).astype(jnp.bfloat16)
    return (query_grad, key_grad, value_grad)


def own_slice(values, col_start, local_width):
    return lax.dynamic_slice_in_dim(values, col_start, local_width, 1)


def shards(
    images,
    cotangent,
    micro_batch,
    heads_weight,
    heads_bias,
    merge_weight,
    merge_bias,
    expand_weight,
    expand_bias,
    shrink_weight,
    shrink_bias,
    norm_gains,
    norm_shifts,
):
    local_width = images.shape[2]
    full_width = local_width * lax.axis_size("col")
    col_start = lax.axis_index("col") * local_width
    local_heads = local_width // HEAD_DIM
    length = images.shape[1]
    slot_count = images.shape[0]
    heads_full, merge_full, expand_full, shrink_full = (
        lax.all_gather(heads_weight, "row", axis=0, tiled=True),
        lax.all_gather(merge_weight, "row", axis=1, tiled=True),
        lax.all_gather(expand_weight, "row", axis=0, tiled=True),
        lax.all_gather(shrink_weight, "row", axis=1, tiled=True),
    )
    member = (micro_batch[:, None] == jnp.arange(MICRO, dtype=jnp.int32)[None, :]).astype(jnp.int32)
    totals = lax.psum(jnp.sum(member, axis=0), ("dp", "row"))
    all_slots = slot_count * lax.axis_size("dp") * lax.axis_size("row")
    batch_weight = all_slots / (MICRO * totals.astype(jnp.float32))
    slot_weight = jnp.sum(member.astype(jnp.float32) * batch_weight[None, :], axis=1)
    gains_own = norm_gains.astype(jnp.float32)
    shifts_own = norm_shifts.astype(jnp.float32)
    heads_bias_own = heads_bias.astype(jnp.float32)
    merge_bias_own = merge_bias.astype(jnp.float32)
    expand_bias_own = expand_bias.astype(jnp.float32)
    shrink_bias_own = shrink_bias.astype(jnp.float32)
    heads_grad = jnp.zeros(heads_full.shape, jnp.float32)
    merge_grad = jnp.zeros(merge_full.shape, jnp.float32)
    expand_grad = jnp.zeros(expand_full.shape, jnp.float32)
    shrink_grad = jnp.zeros(shrink_full.shape, jnp.float32)
    heads_bias_grad = jnp.zeros(heads_bias.shape, jnp.float32)
    merge_bias_grad = jnp.zeros(merge_bias.shape, jnp.float32)
    expand_bias_grad = jnp.zeros(expand_bias.shape, jnp.float32)
    shrink_bias_grad = jnp.zeros(shrink_bias.shape, jnp.float32)
    gain_grad = jnp.zeros(norm_gains.shape, jnp.float32)
    shift_grad = jnp.zeros(norm_shifts.shape, jnp.float32)
    outputs = []
    input_grads = []
    for slot_index in range(slot_count):
        own_input = images[slot_index].astype(jnp.float32)
        weight_now = slot_weight[slot_index]
        normed, centered_one, inverse_one = norm_split(
            own_input, gains_own[0], shifts_own[0], full_width
        )
        mixed_heads = jnp.einsum(
            "td,dkf->tkf", normed, heads_full, preferred_element_type=jnp.float32
        )
        query_low = (
            ((mixed_heads[:, 0] + heads_bias_own[0]) * HEAD_DIM ** (-0.5))
            .astype(jnp.bfloat16)
            .reshape(length, local_heads, HEAD_DIM)
        )
        key_low = mixed_heads[:, 1].astype(jnp.bfloat16).reshape(length, local_heads, HEAD_DIM)
        value_low = (
            (mixed_heads[:, 2] + heads_bias_own[1])
            .astype(jnp.bfloat16)
            .reshape(length, local_heads, HEAD_DIM)
        )
        attended, log_total = attend(query_low, key_low, value_low)
        attended_low = attended.reshape(length, local_width).astype(jnp.bfloat16)
        merge_part = jnp.dot(attended_low, merge_full, preferred_element_type=jnp.float32)
        middle_own = own_input + (branch_split(merge_part) + merge_bias_own)
        normed_two, centered_two, inverse_two = norm_split(
            middle_own, gains_own[1], shifts_own[1], full_width
        )
        hidden = (
            jnp.dot(normed_two, expand_full, preferred_element_type=jnp.float32) + expand_bias_own
        )
        sigmoid_gate = jax.nn.sigmoid(1.702 * hidden)
        activated = (hidden * sigmoid_gate).astype(jnp.bfloat16)
        shrink_part = jnp.dot(activated, shrink_full, preferred_element_type=jnp.float32)
        outputs.append(
            (middle_own + (branch_split(shrink_part) + shrink_bias_own)).astype(jnp.bfloat16)
        )
        cot_full = gather_grads(cotangent[slot_index])
        seed_full = cot_full.astype(jnp.float32) * weight_now
        seed_low = seed_full.astype(jnp.bfloat16)
        seed_own = own_slice(seed_full, col_start, local_width)
        shrink_bias_grad = shrink_bias_grad + jnp.sum(
            own_slice(seed_low, col_start, local_width).astype(jnp.float32), axis=0
        )
        shrink_grad = shrink_grad + jnp.einsum(
            "tf,td->fd", activated, seed_low, preferred_element_type=jnp.float32
        )
        act_grad = jnp.einsum(
            "td,fd->tf", seed_low, shrink_full, preferred_element_type=jnp.float32
        )
        derivative = sigmoid_gate + 1.702 * hidden * sigmoid_gate * (1.0 - sigmoid_gate)
        hidden_grad = (act_grad * derivative).astype(jnp.bfloat16)
        expand_bias_grad = expand_bias_grad + jnp.sum(hidden_grad.astype(jnp.float32), axis=0)
        expand_grad = expand_grad + jnp.einsum(
            "td,tf->df", normed_two, hidden_grad, preferred_element_type=jnp.float32
        )
        norm_part = jnp.einsum(
            "tf,df->td", hidden_grad, expand_full, preferred_element_type=jnp.float32
        )
        norm_result, gain_sum, shift_sum = norm_back_split(
            norm_part, centered_two, inverse_two, gains_own[1], full_width
        )
        middle_grad = seed_own + norm_result
        branch_grad = gather_grads(middle_grad.astype(jnp.bfloat16))
        gain_grad = gain_grad.at[1].add(gain_sum)
        shift_grad = shift_grad.at[1].add(shift_sum)
        merge_bias_grad = merge_bias_grad + jnp.sum(
            own_slice(branch_grad, col_start, local_width).astype(jnp.float32), axis=0
        )
        merge_grad = merge_grad + jnp.einsum(
            "tf,td->fd", attended_low, branch_grad, preferred_element_type=jnp.float32
        )
        attended_grad = (
            jnp.einsum("td,fd->tf", branch_grad, merge_full, preferred_element_type=jnp.float32)
            .astype(jnp.bfloat16)
            .reshape(length, local_heads, HEAD_DIM)
        )
        query_grad, key_grad, value_grad = attend_back(
            query_low, key_low, value_low, log_total, attended_grad
        )
        mixed_grad = jnp.stack(
            [
                query_grad.reshape(length, local_width).astype(jnp.float32) * HEAD_DIM ** (-0.5),
                key_grad.reshape(length, local_width).astype(jnp.float32),
                value_grad.reshape(length, local_width).astype(jnp.float32),
            ],
            axis=1,
        ).astype(jnp.bfloat16)
        heads_bias_grad = heads_bias_grad + jnp.stack(
            [
                jnp.sum(mixed_grad[:, 0].astype(jnp.float32), axis=0),
                jnp.sum(mixed_grad[:, 2].astype(jnp.float32), axis=0),
            ]
        )
        heads_grad = heads_grad + jnp.einsum(
            "td,tkf->dkf", normed, mixed_grad, preferred_element_type=jnp.float32
        )
        first_part = jnp.einsum(
            "tkf,dkf->td", mixed_grad, heads_full, preferred_element_type=jnp.float32
        )
        norm_result, gain_sum, shift_sum = norm_back_split(
            first_part, centered_one, inverse_one, gains_own[0], full_width
        )
        input_grads.append(middle_grad + norm_result)
        gain_grad = gain_grad.at[0].add(gain_sum)
        shift_grad = shift_grad.at[0].add(shift_sum)
    weight_sums = (
        lax.psum_scatter(
            heads_grad.astype(jnp.bfloat16), "row", scatter_dimension=0, tiled=True
        ).astype(jnp.float32),
        lax.psum_scatter(
            merge_grad.astype(jnp.bfloat16), "row", scatter_dimension=1, tiled=True
        ).astype(jnp.float32),
        lax.psum_scatter(
            expand_grad.astype(jnp.bfloat16), "row", scatter_dimension=0, tiled=True
        ).astype(jnp.float32),
        lax.psum_scatter(
            shrink_grad.astype(jnp.bfloat16), "row", scatter_dimension=1, tiled=True
        ).astype(jnp.float32),
    )
    weight_sums = (
        lax.psum(weight_sums[0].astype(jnp.bfloat16), "dp").astype(jnp.float32),
        lax.psum(weight_sums[1].astype(jnp.bfloat16), "dp").astype(jnp.float32),
        lax.psum(weight_sums[2].astype(jnp.bfloat16), "dp").astype(jnp.float32),
        lax.psum(weight_sums[3].astype(jnp.bfloat16), "dp").astype(jnp.float32),
    )
    small_totals = lax.psum(
        (
            heads_bias_grad,
            merge_bias_grad,
            expand_bias_grad,
            shrink_bias_grad,
            gain_grad,
            shift_grad,
        ),
        ("dp", "row"),
    )
    return (
        jnp.stack(outputs),
        jnp.stack(input_grads),
        weight_sums[0],
        small_totals[0],
        weight_sums[1],
        small_totals[1],
        weight_sums[2],
        small_totals[2],
        weight_sums[3],
        small_totals[3],
        small_totals[4],
        small_totals[5],
    )


def solution(mesh):
    placed = (
        P(("dp", "row"), None, "col"),
        P(("dp", "row"), None, "col"),
        P(("dp", "row")),
        P("row", None, "col"),
        P(None, "col"),
        P("col", "row"),
        P("col"),
        P("row", "col"),
        P("col"),
        P("col", "row"),
        P("col"),
        P(None, "col"),
        P(None, "col"),
    )
    return jax.shard_map(
        shards,
        mesh=mesh,
        in_specs=placed,
        out_specs=(
            P(("dp", "row"), None, "col"),
            P(("dp", "row"), None, "col"),
            P("row", None, "col"),
            P(None, "col"),
            P("col", "row"),
            P("col"),
            P("row", "col"),
            P("col"),
            P("col", "row"),
            P("col"),
            P(None, "col"),
            P(None, "col"),
        ),
        check_vma=False,
    )
```

profile of v0, /device:TPU:0, one launch (start us, length us, event | category | flops | bytes accessed | tf_op | source)
XLA Modules:
  0.0 845.2 jit_solution(18113840407815767616)
XLA Ops:
  8.8 4.8 fusion.140
  17.9 3.7 all-reduce.12
  26.4 9.3 %all-gather.35.cloned.1.call-done = bf16[577,1024]{1,0:T(8,128)(2,1)} async-done(((bf16[577,512]{1,0:T(8,128)(2,1)}), bf16[577,1024]{1,0:T(8,128)(2,1)}) %all-gather.35.cloned.1.call-update) | async-done | bytes 1181712 | tf_op jit(solution)/shard_map/all_gather | solution.py:36
  35.7 66.2 %all-gather.25.cloned.1.call-done = bf16[1024,3,512]{2,0,1:T(8,128)(2,1)} async-done(((bf16[256,3,512]{2,0,1:T(8,128)(2,1)}), bf16[1024,3,512]{2,0,1:T(8,128)(2,1)}) %all-gather.25.cloned.1.call-update) | async-done | bytes 3145744 | tf_op jit(solution)/shard_map/all_gather | solution.py:119
  101.9 4.3 fusion.88
  107.9 4.1 all-gather.23.cloned.1.call-done
  112.0 4.3 fusion.92
  122.0 6.5 fusion.145
  132.0 3.2 copy.85
  138.0 6.2 exponential_reduce_fusion
  145.9 4.2 fusion.34
  150.1 3.3 convolution_convert_fusion.3
  153.9 3.4 fusion.144
  166.6 3.7 fusion.139
  173.1 3.4 reduce-scatter.13.cloned.1.call-done
  179.8 3.4 all-reduce.11
  186.0 14.7 %psum.133 = s32[2]{0:T(128)S(1)} all-reduce(s32[2]{0:T(128)S(1)} %fusion.120), channel_id=1, replica_groups=mesh['dp'=4,'row'=4,'col'=2] {'dp','row'}, use_global_device_ids=true, to_apply=%region_17.18 | all-reduce | flops 2 | bytes 16 | tf_op jit(solution)/shard_map/psum | solution.py:125
  201.6 4.2 convert_multiply_fusion.1
  205.7 4.2 convert_multiply_fusion
  210.0 74.1 %all-gather.31.cloned.1.call-done = bf16[1024,2048]{1,0:T(8,128)(2,1)} async-done(((bf16[256,2048]{1,0:T(8,128)(2,1)}), bf16[1024,2048]{1,0:T(8,128)(2,1)}) %all-gather.31.cloned.1.call-update) | async-done | bytes 4194320 | tf_op jit(solution)/shard_map/all_gather | solution.py:121
  284.1 9.2 %all-gather.37.cloned.1.call-done = bf16[577,1024]{1,0:T(8,128)(2,1)} async-done(((bf16[577,512]{1,0:T(8,128)(2,1)}), bf16[577,1024]{1,0:T(8,128)(2,1)}) %all-gather.37.cloned.1.call-update) | async-done | bytes 1181712 | tf_op jit(solution)/shard_map/all_gather | solution.py:36
  293.3 7.4 fusion.147
  300.7 75.9 %all-gather.33.cloned.1.call-done = bf16[2048,1024]{1,0:T(8,128)(2,1)} async-done(((bf16[2048,256]{1,0:T(8,128)(2,1)}), bf16[2048,1024]{1,0:T(8,128)(2,1)}) %all-gather.33.cloned.1.call-update) | async-done | bytes 4194320 | tf_op jit(solution)/shard_map/all_gather | solution.py:122
  376.6 8.6 %convert_reduce_fusion = (f32[2048]{0:T(1024)}, bf16[577,2048]{1,0:T(8,128)(2,1)S(1)}) fusion(f32[577,2048]{1,0:T(8,128)} %fusion.147, f32[2048]{0:T(1024)S(1)} %convert_element_type.388, bf16[2048,1024]{1,0:T(8,128)(2,1)} %all-gather.33.cloned.1.call-done, bf16[1,577,1024]{2,1,0:T(8,128)(2,1)} %get-tuple-element.297), kind=kOutput, calls=%fused_computation.13 | convolution fusion | flops 2435473408 | bytes 12482560 | tf_op jit(solution)/shard_map/td,fd->tf/dot_general | solution.py:193
  386.7 3.7 convolution_convert_fusion
  390.8 4.9 fusion.146
  395.8 4.8 convert_reduce_fusion.1
  402.0 3.7 convolution_convert_fusion.1
  405.8 7.4 convolution_convert_fusion.4
  413.3 7.3 convolution_convert_fusion.2
  420.7 2.9 fusion.78
  423.6 3.7 all-reduce.10
  427.4 3.8 fusion.133
  431.3 5.6 reduce-scatter.19.cloned.1.call-done
  436.9 3.6 fusion.135
  440.6 8.7 %all-gather.39.cloned.1.call-done = bf16[577,1024]{1,0:T(8,128)(2,1)} async-done(((bf16[577,512]{1,0:T(8,128)(2,1)}), bf16[577,1024]{1,0:T(8,128)(2,1)}) %all-gather.39.cloned.1.call-update) | async-done | bytes 1181712 | tf_op jit(solution)/shard_map/all_gather | solution.py:54
  449.4 3.8 fusion.148
  453.1 8.1 all-gather.41.cloned.1.call-done
  461.2 3.9 add_convert_fusion.3
  465.3 5.6 fusion.84
  470.9 8.0 add_convert_fusion
  479.2 5.7 fusion.149
  484.9 5.2 add_convert_fusion.1
  491.5 2.9 convolution_convert_fusion.10
  498.4 7.3 fusion.31
  506.9 7.3 fusion.37
  516.3 6.0 multiply_reduce_fusion
  522.4 6.1 multiply_convert_fusion
  532.1 4.8 fusion.42
  539.2 5.9 multiply_reduce_fusion.1
  545.1 6.2 multiply_convert_fusion.1
  555.0 3.9 fusion.45
  560.0 4.4 fusion.90
  564.5 4.6 add_convert_fusion.2
  569.2 5.4 bitcast_convert_fusion
  574.6 5.3 bitcast_convert_fusion.1
  585.3 65.7 %reduce-scatter.33.cloned.1.call-done = bf16[256,2048]{1,0:T(8,128)(2,1)} async-done(((bf16[1024,2048]{1,0:T(8,128)(2,1)}), bf16[256,2048]{1,0:T(8,128)(2,1)}) %reduce-scatter.33.cloned.1.call-update) | async-done | bytes 1048592 | tf_op jit(solution)/shard_map/reduce_scatter | solution.py:259
  651.0 63.2 %reduce-scatter.29.cloned.1.call-done = bf16[256,3,512]{2,0,1:T(8,128)(2,1)} async-done(((bf16[1024,3,512]{2,0,1:T(8,128)(2,1)}), bf16[256,3,512]{2,0,1:T(8,128)(2,1)}) %reduce-scatter.29.cloned.1.call-update) | async-done | bytes 786448 | tf_op jit(solution)/shard_map/reduce_scatter | solution.py:253
  716.8 9.0 %reduce-scatter.27.cloned.1.call-done = bf16[577,512]{1,0:T(8,128)(2,1)} async-done(((bf16[577,1024]{1,0:T(8,128)(2,1)}), bf16[577,512]{1,0:T(8,128)(2,1)}) %reduce-scatter.27.cloned.1.call-update) | async-done | bytes 590864 | tf_op jit(solution)/shard_map/reduce_scatter | solution.py:40
  725.8 12.6 %reduce-scatter.23.cloned.1.call-done = bf16[577,512]{1,0:T(8,128)(2,1)} async-done(((bf16[577,1024]{1,0:T(8,128)(2,1)}), bf16[577,512]{1,0:T(8,128)(2,1)}) %reduce-scatter.23.cloned.1.call-update) | async-done | bytes 590864 | tf_op jit(solution)/shard_map/reduce_scatter | solution.py:40
  741.2 3.3 all-reduce.9
  747.1 3.2 copy.110
  750.3 78.3 %all-reduce.8 = (f32[2,512]{1,0:T(2,128)}, f32[512]{0:T(512)}, f32[2048]{0:T(1024)}, f32[512]{0:T(512)}, f32[2,512]{1,0:T(2,128)}, /*index=5*/f32[2,512]{1,0:T(2,128)}) all-reduce(f32[2,512]{1,0:T(2,128)S(1)} %maximum_add_fusion, f32[512]{0:T(512)S(1)} %add.530, ...), channel_id=1, replica_groups=mesh['dp'=4,'row'=4,'col'=2] {'dp','row'}, use_global_device_ids=true, to_apply=%region_47.48 | all-reduce | flops 6144 | bytes 49152 | tf_op jit(solution)/shard_map/psum | solution.py:272
  828.6 3.3 all-reduce.16.cloned.1.call-done
  (319 shorter events, 86.9 us)
Async XLA Ops:
  7.2 28.5 %all-gather.35.cloned.1.call-start = ((), (), s32[]{:S(2)}) async-start(), calls=%async_computation.20 | async-start | bytes 1794048 | tf_op jit(solution)/shard_map/all_gather | solution.py:36
  8.0 13.8 %copy-start.55 = (f32[1,512]{1,0:T(1,128)}, f32[1,512]{1,0:T(1,128)S(1)}, u32[]{:S(2)}) copy-start(f32[1,512]{1,0:T(1,128)S(1)} %get-tuple-element.329) | copy-start | bytes 6148
  8.8 4.8 copy-start.70
  23.9 78.1 %all-gather.25.cloned.1.call-start = ((), (), s32[]{:S(2)}) async-start(), calls=%async_computation.13 | async-start | bytes 3932160 | tf_op jit(solution)/shard_map/all_gather | solution.py:119
  24.6 87.4 %all-gather.23.cloned.1.call-start = ((), (), s32[]{:S(2)}) async-start(), calls=%async_computation.12 | async-start | bytes 1794048 | tf_op jit(solution)/shard_map/all_gather | solution.py:36
  25.3 124.7 %all-gather.27.cloned.1.call-start = ((), (), s32[]{:S(2)}) async-start(), calls=%async_computation.14 | async-start | bytes 1310720 | tf_op jit(solution)/shard_map/all_gather | solution.py:120
  25.9 147.2 %reduce-scatter.17.cloned.1.call-start = ((), (), s32[]{:S(2)}) async-start(), calls=%async_computation.21 | async-start | bytes 1794048 | tf_op jit(solution)/shard_map/reduce_scatter | solution.py:58
  26.4 127.5 %copy-start.45 = (f32[8,64]{1,0:T(8,128)}, f32[8,64]{1,0:T(8,128)S(1)}, u32[]{:S(2)}) copy-start(f32[8,64]{1,0:T(8,128)S(1)} %add.478) | copy-start | bytes 6148
  120.0 8.4 copy-start.14
  121.9 6.5 copy-start.10
  130.1 23.8 %copy-start.12 = (bf16[577,1,512]{0,2,1:T(8,128)(2,1)}, bf16[577,1,512]{0,2,1:T(8,128)(2,1)S(1)}, u32[]{:S(2)}) copy-start(bf16[577,1,512]{0,2,1:T(8,128)(2,1)S(1)} %copy.86) | copy-start | bytes 1772548
  132.0 27.0 %copy-start.6 = (f32[577,1,512]{0,2,1:T(8,128)}, f32[577,1,512]{0,2,1:T(8,128)S(1)}, u32[]{:S(2)}) copy-start(f32[577,1,512]{0,2,1:T(8,128)S(1)} %copy.84) | copy-start | bytes 3545092
  138.0 7.9 copy-start
  153.4 23.1 %reduce-scatter.13.cloned.1.call-start = ((), (), s32[]{:S(2)}) async-start(), calls=%async_computation.15 | async-start | bytes 1794048 | tf_op jit(solution)/shard_map/reduce_scatter | solution.py:58
  166.5 35.0 %all-gather.43.cloned.1.call-start = ((), (), s32[]{:S(2)}) async-start(), calls=%async_computation.34 | async-start | bytes 1794048 | tf_op jit(solution)/shard_map/all_gather | solution.py:54
  171.2 34.5 %all-gather.45.cloned.1.call-start = ((), (), s32[]{:S(2)}) async-start(), calls=%async_computation.35 | async-start | bytes 1794048 | tf_op jit(solution)/shard_map/all_gather | solution.py:54
  172.3 111.8 %all-gather.31.cloned.1.call-start = ((), (), s32[]{:S(2)}) async-start(), calls=%async_computation.17 | async-start | bytes 5242880 | tf_op jit(solution)/shard_map/all_gather | solution.py:121
  173.0 120.3 %all-gather.37.cloned.1.call-start = ((), (), s32[]{:S(2)}) async-start(), calls=%async_computation.22 | async-start | bytes 1794048 | tf_op jit(solution)/shard_map/all_gather | solution.py:36
  173.1 5.4 copy-start.4
  185.1 15.6 %copy-start.59 = (bf16[2048]{0:T(1024)(128)(2,1)S(1)}, bf16[2048]{0:T(1024)(128)(2,1)}, u32[]{:S(2)}) copy-start(bf16[2048]{0:T(1024)(128)(2,1)} %param.37) | copy-start | bytes 12292
  185.2 191.4 %all-gather.33.cloned.1.call-start = ((), (), s32[]{:S(2)}) async-start(), calls=%async_computation.18 | async-start | bytes 5242880 | tf_op jit(solution)/shard_map/all_gather | solution.py:122
  185.9 204.9 %all-gather.29.cloned.1.call-start = ((), (), s32[]{:S(2)}) async-start(), calls=%async_computation.16 | async-start | bytes 1794048 | tf_op jit(solution)/shard_map/all_gather | solution.py:36
  210.0 210.8 %reduce-scatter.25.cloned.1.call-start = ((), (), s32[]{:S(2)}) async-start(), calls=%async_computation.27 | async-start | bytes 1794048 | tf_op jit(solution)/shard_map/reduce_scatter | solution.py:40
  376.6 10.1 %copy-start.63 = (bf16[1024,2048]{1,0:T(8,128)(2,1)S(1)}, bf16[1024,2048]{1,0:T(8,128)(2,1)}, u32[]{:S(2)}) copy-start(bf16[1024,2048]{1,0:T(8,128)(2,1)} %all-gather.31.cloned.1.call-done) | copy-start | bytes 12582916
  390.5 30.2 %reduce-scatter.21.cloned.1.call-start = ((), (), s32[]{:S(2)}) async-start(), calls=%async_computation.24 | async-start | bytes 1794048 | tf_op jit(solution)/shard_map/reduce_scatter | solution.py:40
  390.8 5.0 copy-start.23
  390.8 5.0 copy-start.65
  395.7 4.9 copy-start.71
  395.8 6.3 copy-start.64
  405.8 21.6 %reduce-scatter.15.cloned.1.call-start = ((), (), s32[]{:S(2)}) async-start(), calls=%async_computation.19 | async-start | bytes 1794048 | tf_op jit(solution)/shard_map/reduce_scatter | solution.py:58
  413.2 7.5 copy-start.62
  413.2 23.7 %reduce-scatter.19.cloned.1.call-start = ((), (), s32[]{:S(2)}) async-start(), calls=%async_computation.23 | async-start | bytes 1794048 | tf_op jit(solution)/shard_map/reduce_scatter | solution.py:58
  420.6 28.7 %all-gather.39.cloned.1.call-start = ((), (), s32[]{:S(2)}) async-start(), calls=%async_computation.25 | async-start | bytes 1794048 | tf_op jit(solution)/shard_map/all_gather | solution.py:54
  427.4 9.5 %copy-start.32 = (bf16[577,512]{1,0:T(8,128)(2,1)S(1)}, bf16[577,512]{1,0:T(8,128)(2,1)}, u32[]{:S(2)}) copy-start(bf16[577,512]{1,0:T(8,128)(2,1)} %reduce-scatter.25.cloned.1.call-done) | copy-start | bytes 1772548
  431.2 30.0 %all-gather.41.cloned.1.call-start = ((), (), s32[]{:S(2)}) async-start(), calls=%async_computation.28 | async-start | bytes 1794048 | tf_op jit(solution)/shard_map/all_gather | solution.py:54
  440.6 20.7 %copy-start.28 = (bf16[8,64,577]{2,1,0:T(8,128)(2,1)S(1)}, bf16[8,64,577]{2,1,0:T(8,128)(2,1)}, u32[]{:S(2)}) copy-start(bf16[8,64,577]{2,1,0:T(8,128)(2,1)} %fusion.34) | copy-start | bytes 1772548
  440.6 144.7 %reduce-scatter.31.cloned.1.call-start = ((), (), s32[]{:S(2)}) async-start(), calls=%async_computation.31 | async-start | bytes 1310720 | tf_op jit(solution)/shard_map/reduce_scatter | solution.py:256
  453.1 12.1 %copy-start.24 = (bf16[1,577,1024]{2,1,0:T(8,128)(2,1)S(1)}, bf16[1,577,1024]{2,1,0:T(8,128)(2,1)}, u32[]{:S(2)}) copy-start(bf16[1,577,1024]{2,1,0:T(8,128)(2,1)} %get-tuple-element.295) | copy-start | bytes 3545092
  465.2 120.1 %reduce-scatter.35.cloned.1.call-start = ((), (), s32[]{:S(2)}) async-start(), calls=%async_computation.33 | async-start | bytes 5242880 | tf_op jit(solution)/shard_map/reduce_scatter | solution.py:262
  465.2 5.6 copy-start.25
  478.9 6.0 copy-start.67
  479.0 172.0 %reduce-scatter.33.cloned.1.call-start = ((), (), s32[]{:S(2)}) async-start(), calls=%async_computation.32 | async-start | bytes 5242880 | tf_op jit(solution)/shard_map/reduce_scatter | solution.py:259
  479.2 5.8 copy-start.74
  490.2 223.9 %reduce-scatter.29.cloned.1.call-start = ((), (), s32[]{:S(2)}) async-start(), calls=%async_computation.30 | async-start | bytes 3932160 | tf_op jit(solution)/shard_map/reduce_scatter | solution.py:253
  498.4 7.3 copy-start.17
  498.4 8.4 copy-start.43
  506.9 9.5 %copy-start.8 = (f32[577,1,512]{0,2,1:T(8,128)S(1)}, f32[577,1,512]{0,2,1:T(8,128)}, u32[]{:S(2)}) copy-start(f32[577,1,512]{0,2,1:T(8,128)} %copy.89) | copy-start | bytes 3545092
  522.4 6.1 copy-start.11
  522.4 6.1 copy-start.46
  532.1 7.1 copy-start.7
  545.1 6.2 copy-start.9
  555.0 5.0 copy-start.38
  560.0 4.5 copy-start.41
  560.0 4.5 copy-start.66
  569.1 156.7 %reduce-scatter.27.cloned.1.call-start = ((), (), s32[]{:S(2)}) async-start(), calls=%async_computation.29 | async-start | bytes 1794048 | tf_op jit(solution)/shard_map/reduce_scatter | solution.py:40
  574.6 163.8 %reduce-scatter.23.cloned.1.call-start = ((), (), s32[]{:S(2)}) async-start(), calls=%async_computation.26 | async-start | bytes 1794048 | tf_op jit(solution)/shard_map/reduce_scatter | solution.py:40
  580.0 251.9 %all-reduce.16.cloned.1.call-start = ((), (), s32[]{:S(2)}) async-start(), calls=%async_computation.36 | async-start | bytes 6291456 | tf_op jit(solution)/shard_map/psum | solution.py:267
  715.2 23.2 %copy-start.48 = (f32[577]{0:T(1024)S(1)}, f32[577]{0:T(1024)}, u32[]{:S(2)}) copy-start(f32[577]{0:T(1024)} %copy-done.47) | copy-start | bytes 6928
  715.2 23.2 %copy-start.50 = (f32[577]{0:T(1024)S(1)}, f32[577]{0:T(1024)}, u32[]{:S(2)}) copy-start(f32[577]{0:T(1024)} %copy-done.49) | copy-start | bytes 6928
  715.2 23.2 %copy-start.52 = (f32[577]{0:T(1024)S(1)}, f32[577]{0:T(1024)}, u32[]{:S(2)}) copy-start(f32[577]{0:T(1024)} %copy-done.51) | copy-start | bytes 6928
  715.2 23.2 %copy-start.54 = (f32[577]{0:T(1024)S(1)}, f32[577]{0:T(1024)}, u32[]{:S(2)}) copy-start(f32[577]{0:T(1024)} %copy-done.53) | copy-start | bytes 6928
  715.3 23.2 %copy-start.56 = (f32[1,512]{1,0:T(1,128)S(1)}, f32[1,512]{1,0:T(1,128)}, u32[]{:S(2)}) copy-start(f32[1,512]{1,0:T(1,128)} %copy-done.55) | copy-start | bytes 6148
  716.7 27.9 %copy-start.22 = (f32[577,512]{1,0:T(8,128)S(1)}, f32[577,512]{1,0:T(8,128)}, u32[]{:S(2)}) copy-start(f32[577,512]{1,0:T(8,128)} %get-tuple-element.281) | copy-start | bytes 3545092
  725.8 18.8 %copy-start.33 = (bf16[577,512]{1,0:T(8,128)(2,1)S(1)}, bf16[577,512]{1,0:T(8,128)(2,1)}, u32[]{:S(2)}) copy-start(bf16[577,512]{1,0:T(8,128)(2,1)} %reduce-scatter.27.cloned.1.call-done) | copy-start | bytes 1772548
  (36 other events, 71.9 us)
Sparse Core Ops, SparseCore 0:
  24.0 11.6 all-gather.34
  37.3 64.6 all-gather.24
  104.0 7.9 all-gather.22
  113.4 31.3 all-gather.26
  153.5 9.7 reduce-scatter.16
  166.7 9.8 reduce-scatter.12
  178.1 10.4 all-gather.42
  190.1 10.4 all-gather.44
  202.1 81.9 all-gather.30
  285.5 7.7 all-gather.36
  294.8 81.7 all-gather.32
  378.6 7.4 all-gather.28
  390.6 7.4 reduce-scatter.24
  405.9 6.8 reduce-scatter.20
  414.9 9.8 reduce-scatter.14
  427.0 9.8 reduce-scatter.18
  438.9 10.4 all-gather.38
  450.8 10.4 all-gather.40
  465.3 28.3 reduce-scatter.30
  495.9 75.4 reduce-scatter.34
  573.7 77.2 reduce-scatter.32
  653.4 60.7 reduce-scatter.28
  717.1 8.6 reduce-scatter.26
  728.5 9.8 reduce-scatter.22
  742.1 89.7 all-reduce.15
where the time goes:
time: 851 us; the launch traced here: 845 us
  waiting for transfers between devices  422 us (50%)
  matrix products  174 us (20%)
  blocking collectives  107 us (13%)
  other arithmetic  63.1 us (7%)
  local copies, waits for them, and re-layouts  60.1 us (7%)
  between operations  16.3 us (2%)
    psum x1, blocking collectives, shards(): lax.psum((heads_bias_grad, merge_bias_grad, expand_bias_grad, shrink_bias...  78.3 us
    all_gather x1, waiting for transfers between devices, shards(): lax.all_gather(shrink_weight, 'row', axis=1, tiled=True)  75.9 us
    all_gather x1, waiting for transfers between devices, shards(): lax.all_gather(expand_weight, 'row', axis=0, tiled=True)  74.1 us
    all_gather x1, waiting for transfers between devices, shards(): lax.all_gather(heads_weight, 'row', axis=0, tiled=True)  66.2 us
    reduce_scatter x1, waiting for transfers between devices, shards(): lax.psum_scatter(expand_grad.astype(jnp.bfloat16), 'row', scatter_dimensi...  65.7 us
    reduce_scatter x1, waiting for transfers between devices, shards(): lax.psum_scatter(heads_grad.astype(jnp.bfloat16), 'row', scatter_dimensio...  63.2 us
    unnamed x167, local copies, waits for them, and re-layouts  23.8 us
    all_gather x4, waiting for transfers between devices, norm_split(): lax.all_gather(normed, 'col', axis=1, tiled=True)  22.7 us
  transfers between devices with their start and end apart: 25, of which 15 were waited for; matrix products, arithmetic and copies ran while one was open for 30% of the time, Pallas kernels for 0%

commit v1 on v0

--- a/solution.py
+++ b/solution.py
@@ -115,10 +115,19 @@
     local_heads = local_width // HEAD_DIM
     length = images.shape[1]
     slot_count = images.shape[0]
+    create_the_screen = lambda inner_x: jnp.concatenate(
+        lax.all_to_all(
+            jnp.stack([inner_x] * lax.axis_size("row")),
+            axis_name="row",
+            split_axis=0,
+            concat_axis=0,
+        ),
+        axis=0,
+    )
     heads_full, merge_full, expand_full, shrink_full = (
         lax.all_gather(heads_weight, "row", axis=0, tiled=True),
         lax.all_gather(merge_weight, "row", axis=1, tiled=True),
-        lax.all_gather(expand_weight, "row", axis=0, tiled=True),
+        create_the_screen(expand_weight),
         lax.all_gather(shrink_weight, "row", axis=1, tiled=True),
     )
     member = (micro_batch[:, None] == jnp.arange(MICRO, dtype=jnp.int32)[None, :]).astype(jnp.int32)

time: 851 us -> 854 us (level)
  waiting for transfers between devices: 422 us -> 261 us
  blocking collectives: 107 us -> 258 us
    psum x1, blocking collectives: 14.7 us -> 165 us  [shards(): totals = lax.psum(jnp.sum(member, axis=0), ('dp', 'row'))]
    all_gather x1, waiting for transfers between devices: 75.9 us -> 0.01 us  [shards(): lax.all_gather(shrink_weight, 'row', axis=1, tiled=True)]
    all_gather x1 -> x0, waiting for transfers between devices: 74.1 us -> none  [shards(): lax.all_gather(expand_weight, 'row', axis=0, tiled=True)]
    all_gather x4, waiting for transfers between devices: 22.7 us -> 13.5 us  [norm_split(): lax.all_gather(normed, 'col', axis=1, tiled=True)]
    unnamed x167 -> x169, local copies, waits for them, and re-layouts: 23.8 us -> 24.4 us
  transfers between devices with their start and end apart: 25 -> 25, of which waited for: 15 -> 12; matrix products, arithmetic and copies ran while one was open for 30% -> 31% of each run, Pallas kernels for 0% -> 0%
where the time goes in v1:
time: 854 us; the launch traced here: 848 us
  waiting for transfers between devices  261 us (31%)
  blocking collectives  258 us (30%)
  matrix products  179 us (21%)
  local copies, waits for them, and re-layouts  63.3 us (7%)
  other arithmetic  63 us (7%)
  between operations  16.6 us (2%)
    psum x1, blocking collectives, shards(): totals = lax.psum(jnp.sum(member, axis=0), ('dp', 'row'))  165 us
    psum x1, blocking collectives, shards(): lax.psum((heads_bias_grad, merge_bias_grad, expand_bias_grad, shrink_bias...  78.2 us
    all_gather x1, waiting for transfers between devices, shards(): lax.all_gather(heads_weight, 'row', axis=0, tiled=True)  66.2 us
    reduce_scatter x1, waiting for transfers between devices, shards(): lax.psum_scatter(expand_grad.astype(jnp.bfloat16), 'row', scatter_dimensi...  65.7 us
    reduce_scatter x1, waiting for transfers between devices, shards(): lax.psum_scatter(heads_grad.astype(jnp.bfloat16), 'row', scatter_dimensio...  63.2 us
    unnamed x169, local copies, waits for them, and re-layouts  24.4 us
    reduce_scatter x4, waiting for transfers between devices, norm_back_split(): lax.psum_scatter(partial_rows.astype(jnp.bfloat16), 'col', scatter_dimens...  21.8 us
  transfers between devices with their start and end apart: 25, of which 12 were waited for; matrix products, arithmetic and copies ran while one was open for 31% of the time, Pallas kernels for 0%

profile of v1, /device:TPU:0, one launch (start us, length us, event | category | flops | bytes accessed | tf_op | source)
XLA Modules:
  0.0 847.7 jit_solution(6610414985704828692)
XLA Ops:
  8.8 4.8 fusion.140
  17.9 3.7 all-reduce.12
  26.4 9.3 %all-gather.32.cloned.1.call-done = bf16[577,1024]{1,0:T(8,128)(2,1)} async-done(((bf16[577,512]{1,0:T(8,128)(2,1)}), bf16[577,1024]{1,0:T(8,128)(2,1)}) %all-gather.32.cloned.1.call-update) | async-done | bytes 1181712 | tf_op jit(solution)/shard_map/all_gather | solution.py:36
  35.7 66.2 %all-gather.24.cloned.1.call-done = bf16[1024,3,512]{2,0,1:T(8,128)(2,1)} async-done(((bf16[256,3,512]{2,0,1:T(8,128)(2,1)}), bf16[1024,3,512]{2,0,1:T(8,128)(2,1)}) %all-gather.24.cloned.1.call-update) | async-done | bytes 3145744 | tf_op jit(solution)/shard_map/all_gather | solution.py:128
  101.9 4.3 fusion.88
  107.9 4.1 all-gather.22.cloned.1.call-done
  112.0 4.3 fusion.92
  122.0 6.5 fusion.145
  132.0 3.2 copy.85
  135.3 2.7 copy.89
  138.0 6.2 exponential_reduce_fusion
  145.9 4.2 fusion.34
  150.1 3.3 convolution_convert_fusion.3
  153.9 3.4 fusion.144
  159.1 2.7 copy-done.1
  166.6 3.7 fusion.139
  172.4 4.1 reduce-scatter.13.cloned.1.call-done
  179.8 3.5 all-reduce.11
  189.0 5.1 all-to-all-start
  194.2 165.4 %psum.133 = s32[2]{0:T(128)S(1)} all-reduce(s32[2]{0:T(128)S(1)} %fusion.120), channel_id=1, replica_groups=mesh['dp'=4,'row'=4,'col'=2] {'dp','row'}, use_global_device_ids=true, to_apply=%region_17.18 | all-reduce | flops 2 | bytes 16 | tf_op jit(solution)/shard_map/psum | solution.py:134
  360.4 4.2 convert_multiply_fusion.1
  364.6 4.2 convert_multiply_fusion
  368.9 7.5 fusion.147
  376.4 8.5 %convert_reduce_fusion = (f32[2048]{0:T(1024)}, bf16[577,2048]{1,0:T(8,128)(2,1)S(1)}) fusion(f32[577,2048]{1,0:T(8,128)} %fusion.147, f32[2048]{0:T(1024)S(1)} %convert_element_type.388, bf16[2048,1024]{1,0:T(8,128)(2,1)} %all-gather.30.cloned.1.call-done, bf16[1,577,1024]{2,1,0:T(8,128)(2,1)} %get-tuple-element.297), kind=kOutput, calls=%fused_computation.13 | convolution fusion | flops 2435473408 | bytes 12482560 | tf_op jit(solution)/shard_map/td,fd->tf/dot_general | solution.py:202
  386.4 6.0 convolution_convert_fusion
  392.7 5.0 fusion.146
  397.8 4.8 convert_reduce_fusion.1
  404.0 6.0 convolution_convert_fusion.1
  410.1 7.7 convolution_convert_fusion.4
  417.9 7.3 convolution_convert_fusion.2
  425.4 2.9 fusion.78
  428.3 3.7 all-reduce.10
  432.0 3.8 fusion.133
  435.9 3.2 reduce-scatter.19.cloned.1.call-done
  439.2 3.5 fusion.135
  442.8 8.8 %all-gather.36.cloned.1.call-done = bf16[577,1024]{1,0:T(8,128)(2,1)} async-done(((bf16[577,512]{1,0:T(8,128)(2,1)}), bf16[577,1024]{1,0:T(8,128)(2,1)}) %all-gather.36.cloned.1.call-update) | async-done | bytes 1181712 | tf_op jit(solution)/shard_map/all_gather | solution.py:54
  451.6 3.8 fusion.148
  455.4 8.1 all-gather.38.cloned.1.call-done
  463.5 3.9 add_convert_fusion.3
  467.5 5.6 fusion.84
  473.1 8.0 add_convert_fusion
  481.4 5.7 fusion.149
  487.2 5.2 add_convert_fusion.1
  493.7 2.9 convolution_convert_fusion.10
  500.7 7.3 fusion.31
  509.1 7.3 fusion.37
  518.6 6.0 multiply_reduce_fusion
  524.7 6.1 multiply_convert_fusion
  534.4 4.8 fusion.42
  541.4 5.9 multiply_reduce_fusion.1
  547.4 6.1 multiply_convert_fusion.1
  557.2 3.9 fusion.45
  562.2 4.4 fusion.90
  566.7 4.6 add_convert_fusion.2
  571.4 5.3 bitcast_convert_fusion
  576.8 5.3 bitcast_convert_fusion.1
  587.5 65.7 %reduce-scatter.33.cloned.1.call-done = bf16[256,2048]{1,0:T(8,128)(2,1)} async-done(((bf16[1024,2048]{1,0:T(8,128)(2,1)}), bf16[256,2048]{1,0:T(8,128)(2,1)}) %reduce-scatter.33.cloned.1.call-update) | async-done | bytes 1048592 | tf_op jit(solution)/shard_map/reduce_scatter | solution.py:268
  653.2 63.2 %reduce-scatter.29.cloned.1.call-done = bf16[256,3,512]{2,0,1:T(8,128)(2,1)} async-done(((bf16[1024,3,512]{2,0,1:T(8,128)(2,1)}), bf16[256,3,512]{2,0,1:T(8,128)(2,1)}) %reduce-scatter.29.cloned.1.call-update) | async-done | bytes 786448 | tf_op jit(solution)/shard_map/reduce_scatter | solution.py:262
  719.0 9.0 %reduce-scatter.27.cloned.1.call-done = bf16[577,512]{1,0:T(8,128)(2,1)} async-done(((bf16[577,1024]{1,0:T(8,128)(2,1)}), bf16[577,512]{1,0:T(8,128)(2,1)}) %reduce-scatter.27.cloned.1.call-update) | async-done | bytes 590864 | tf_op jit(solution)/shard_map/reduce_scatter | solution.py:40
  728.0 12.7 %reduce-scatter.23.cloned.1.call-done = bf16[577,512]{1,0:T(8,128)(2,1)} async-done(((bf16[577,1024]{1,0:T(8,128)(2,1)}), bf16[577,512]{1,0:T(8,128)(2,1)}) %reduce-scatter.23.cloned.1.call-update) | async-done | bytes 590864 | tf_op jit(solution)/shard_map/reduce_scatter | solution.py:40
  743.6 3.3 all-reduce.9
  749.5 3.2 copy.110
  752.7 78.2 %all-reduce.8 = (f32[2,512]{1,0:T(2,128)}, f32[512]{0:T(512)}, f32[2048]{0:T(1024)}, f32[512]{0:T(512)}, f32[2,512]{1,0:T(2,128)}, /*index=5*/f32[2,512]{1,0:T(2,128)}) all-reduce(f32[2,512]{1,0:T(2,128)S(1)} %maximum_add_fusion, f32[512]{0:T(512)S(1)} %add.530, ...), channel_id=1, replica_groups=mesh['dp'=4,'row'=4,'col'=2] {'dp','row'}, use_global_device_ids=true, to_apply=%region_47.48 | all-reduce | flops 6144 | bytes 49152 | tf_op jit(solution)/shard_map/psum | solution.py:281
  830.9 3.2 all-reduce.16.cloned.1.call-done
  (321 shorter events, 83.8 us)
Async XLA Ops:
  7.2 28.5 %all-gather.32.cloned.1.call-start = ((), (), s32[]{:S(2)}) async-start(), calls=%async_computation.20 | async-start | bytes 1794048 | tf_op jit(solution)/shard_map/all_gather | solution.py:36
  8.0 13.8 %copy-start.58 = (f32[1,512]{1,0:T(1,128)}, f32[1,512]{1,0:T(1,128)S(1)}, u32[]{:S(2)}) copy-start(f32[1,512]{1,0:T(1,128)S(1)} %get-tuple-element.329) | copy-start | bytes 6148
  8.8 4.8 copy-start.71
  23.9 78.1 %all-gather.24.cloned.1.call-start = ((), (), s32[]{:S(2)}) async-start(), calls=%async_computation.14 | async-start | bytes 3932160 | tf_op jit(solution)/shard_map/all_gather | solution.py:128
  24.6 87.4 %all-gather.22.cloned.1.call-start = ((), (), s32[]{:S(2)}) async-start(), calls=%async_computation.13 | async-start | bytes 1794048 | tf_op jit(solution)/shard_map/all_gather | solution.py:36
  25.3 124.7 %all-gather.26.cloned.1.call-start = ((), (), s32[]{:S(2)}) async-start(), calls=%async_computation.15 | async-start | bytes 1310720 | tf_op jit(solution)/shard_map/all_gather | solution.py:129
  25.9 146.4 %reduce-scatter.17.cloned.1.call-start = ((), (), s32[]{:S(2)}) async-start(), calls=%async_computation.21 | async-start | bytes 1794048 | tf_op jit(solution)/shard_map/reduce_scatter | solution.py:58
  26.3 132.7 %copy-start.48 = (f32[8,64]{1,0:T(8,128)}, f32[8,64]{1,0:T(8,128)S(1)}, u32[]{:S(2)}) copy-start(f32[8,64]{1,0:T(8,128)S(1)} %add.475) | copy-start | bytes 6148
  26.4 127.5 %copy-start.46 = (f32[8,64]{1,0:T(8,128)}, f32[8,64]{1,0:T(8,128)S(1)}, u32[]{:S(2)}) copy-start(f32[8,64]{1,0:T(8,128)S(1)} %add.478) | copy-start | bytes 6148
  120.0 8.4 copy-start.14
  122.0 6.5 copy-start.10
  130.1 23.8 %copy-start.12 = (bf16[577,1,512]{0,2,1:T(8,128)(2,1)}, bf16[577,1,512]{0,2,1:T(8,128)(2,1)S(1)}, u32[]{:S(2)}) copy-start(bf16[577,1,512]{0,2,1:T(8,128)(2,1)S(1)} %copy.86) | copy-start | bytes 1772548
  132.0 27.0 %copy-start.6 = (f32[577,1,512]{0,2,1:T(8,128)}, f32[577,1,512]{0,2,1:T(8,128)S(1)}, u32[]{:S(2)}) copy-start(f32[577,1,512]{0,2,1:T(8,128)S(1)} %copy.84) | copy-start | bytes 3545092
  138.0 7.9 copy-start
  153.4 23.1 %reduce-scatter.13.cloned.1.call-start = ((), (), s32[]{:S(2)}) async-start(), calls=%async_computation.16 | async-start | bytes 1794048 | tf_op jit(solution)/shard_map/reduce_scatter | solution.py:58
  166.5 193.9 %all-gather.40.cloned.1.call-start = ((), (), s32[]{:S(2)}) async-start(), calls=%async_computation.34 | async-start | bytes 1794048 | tf_op jit(solution)/shard_map/all_gather | solution.py:54
  171.2 193.3 %all-gather.42.cloned.1.call-start = ((), (), s32[]{:S(2)}) async-start(), calls=%async_computation.35 | async-start | bytes 1794048 | tf_op jit(solution)/shard_map/all_gather | solution.py:54
  172.3 196.6 %all-gather.34.cloned.1.call-start = ((), (), s32[]{:S(2)}) async-start(), calls=%async_computation.22 | async-start | bytes 1794048 | tf_op jit(solution)/shard_map/all_gather | solution.py:36
  172.4 6.1 copy-start.4
  185.2 191.2 %all-gather.30.cloned.1.call-start = ((), (), s32[]{:S(2)}) async-start(), calls=%async_computation.18 | async-start | bytes 5242880 | tf_op jit(solution)/shard_map/all_gather | solution.py:131
  189.0 5.1 copy-start.70
  189.0 170.6 %copy-start.62 = (bf16[2048]{0:T(1024)(128)(2,1)S(1)}, bf16[2048]{0:T(1024)(128)(2,1)}, u32[]{:S(2)}) copy-start(bf16[2048]{0:T(1024)(128)(2,1)} %param.37) | copy-start | bytes 12292
  189.0 179.8 %all-to-all-start = ((bf16[4,256,2048]{2,1,0:T(8,128)(2,1)}), bf16[4,256,2048]{2,1,0:T(8,128)(2,1)}, u32[]{:S(2)}, u32[]{:S(2)}) async-start(bf16[4,256,2048]{2,1,0:T(8,128)(2,1)} %stack.57), calls=%async_computation.1 | async-start | bytes 8388608 | tf_op jit(solution)/shard_map/all_to_all | solution.py:119
  194.1 198.6 %all-gather.28.cloned.1.call-start = ((), (), s32[]{:S(2)}) async-start(), calls=%async_computation.17 | async-start | bytes 1794048 | tf_op jit(solution)/shard_map/all_gather | solution.py:36
  368.8 56.6 %reduce-scatter.25.cloned.1.call-start = ((), (), s32[]{:S(2)}) async-start(), calls=%async_computation.27 | async-start | bytes 1794048 | tf_op jit(solution)/shard_map/reduce_scatter | solution.py:40
  392.4 32.9 %reduce-scatter.21.cloned.1.call-start = ((), (), s32[]{:S(2)}) async-start(), calls=%async_computation.24 | async-start | bytes 1794048 | tf_op jit(solution)/shard_map/reduce_scatter | solution.py:40
  392.7 5.0 copy-start.23
  392.7 5.0 copy-start.66
  397.7 4.9 copy-start.72
  410.0 22.0 %reduce-scatter.15.cloned.1.call-start = ((), (), s32[]{:S(2)}) async-start(), calls=%async_computation.19 | async-start | bytes 1794048 | tf_op jit(solution)/shard_map/reduce_scatter | solution.py:58
  417.8 7.5 copy-start.65
  417.8 21.3 %reduce-scatter.19.cloned.1.call-start = ((), (), s32[]{:S(2)}) async-start(), calls=%async_computation.23 | async-start | bytes 1794048 | tf_op jit(solution)/shard_map/reduce_scatter | solution.py:58
  425.3 26.4 %all-gather.36.cloned.1.call-start = ((), (), s32[]{:S(2)}) async-start(), calls=%async_computation.25 | async-start | bytes 1794048 | tf_op jit(solution)/shard_map/all_gather | solution.py:54
  432.0 7.1 copy-start.32
  435.9 27.6 %all-gather.38.cloned.1.call-start = ((), (), s32[]{:S(2)}) async-start(), calls=%async_computation.28 | async-start | bytes 1794048 | tf_op jit(solution)/shard_map/all_gather | solution.py:54
  442.7 20.7 %copy-start.28 = (bf16[8,64,577]{2,1,0:T(8,128)(2,1)S(1)}, bf16[8,64,577]{2,1,0:T(8,128)(2,1)}, u32[]{:S(2)}) copy-start(bf16[8,64,577]{2,1,0:T(8,128)(2,1)} %fusion.34) | copy-start | bytes 1772548
  442.7 144.7 %reduce-scatter.31.cloned.1.call-start = ((), (), s32[]{:S(2)}) async-start(), calls=%async_computation.31 | async-start | bytes 1310720 | tf_op jit(solution)/shard_map/reduce_scatter | solution.py:265
  455.4 12.1 %copy-start.24 = (bf16[1,577,1024]{2,1,0:T(8,128)(2,1)S(1)}, bf16[1,577,1024]{2,1,0:T(8,128)(2,1)}, u32[]{:S(2)}) copy-start(bf16[1,577,1024]{2,1,0:T(8,128)(2,1)} %get-tuple-element.295) | copy-start | bytes 3545092
  467.4 120.0 %reduce-scatter.35.cloned.1.call-start = ((), (), s32[]{:S(2)}) async-start(), calls=%async_computation.33 | async-start | bytes 5242880 | tf_op jit(solution)/shard_map/reduce_scatter | solution.py:271
  467.5 5.7 copy-start.25
  481.2 6.0 copy-start.68
  481.2 172.0 %reduce-scatter.33.cloned.1.call-start = ((), (), s32[]{:S(2)}) async-start(), calls=%async_computation.32 | async-start | bytes 5242880 | tf_op jit(solution)/shard_map/reduce_scatter | solution.py:268
  481.4 5.8 copy-start.75
  492.4 223.9 %reduce-scatter.29.cloned.1.call-start = ((), (), s32[]{:S(2)}) async-start(), calls=%async_computation.30 | async-start | bytes 3932160 | tf_op jit(solution)/shard_map/reduce_scatter | solution.py:262
  500.7 7.3 copy-start.17
  500.7 8.4 copy-start.44
  509.1 9.5 %copy-start.8 = (f32[577,1,512]{0,2,1:T(8,128)S(1)}, f32[577,1,512]{0,2,1:T(8,128)}, u32[]{:S(2)}) copy-start(f32[577,1,512]{0,2,1:T(8,128)} %copy.89) | copy-start | bytes 3545092
  509.1 9.5 %copy-start.49 = (f32[8,64]{1,0:T(8,128)S(1)}, f32[8,64]{1,0:T(8,128)}, u32[]{:S(2)}) copy-start(f32[8,64]{1,0:T(8,128)} %copy-done.48) | copy-start | bytes 6148
  524.6 6.1 copy-start.11
  524.6 6.1 copy-start.47
  534.4 7.0 copy-start.7
  547.3 6.2 copy-start.9
  557.2 5.0 copy-start.39
  562.2 4.5 copy-start.67
  571.4 156.7 %reduce-scatter.27.cloned.1.call-start = ((), (), s32[]{:S(2)}) async-start(), calls=%async_computation.29 | async-start | bytes 1794048 | tf_op jit(solution)/shard_map/reduce_scatter | solution.py:40
  576.8 164.0 %reduce-scatter.23.cloned.1.call-start = ((), (), s32[]{:S(2)}) async-start(), calls=%async_computation.26 | async-start | bytes 1794048 | tf_op jit(solution)/shard_map/reduce_scatter | solution.py:40
  582.2 251.9 %all-reduce.16.cloned.1.call-start = ((), (), s32[]{:S(2)}) async-start(), calls=%async_computation.36 | async-start | bytes 6291456 | tf_op jit(solution)/shard_map/psum | solution.py:276
  717.5 23.3 %copy-start.51 = (f32[577]{0:T(1024)S(1)}, f32[577]{0:T(1024)}, u32[]{:S(2)}) copy-start(f32[577]{0:T(1024)} %copy-done.50) | copy-start | bytes 6928
  717.5 23.3 %copy-start.53 = (f32[577]{0:T(1024)S(1)}, f32[577]{0:T(1024)}, u32[]{:S(2)}) copy-start(f32[577]{0:T(1024)} %copy-done.52) | copy-start | bytes 6928
  717.5 23.3 %copy-start.55 = (f32[577]{0:T(1024)S(1)}, f32[577]{0:T(1024)}, u32[]{:S(2)}) copy-start(f32[577]{0:T(1024)} %copy-done.54) | copy-start | bytes 6928
  717.5 23.3 %copy-start.57 = (f32[577]{0:T(1024)S(1)}, f32[577]{0:T(1024)}, u32[]{:S(2)}) copy-start(f32[577]{0:T(1024)} %copy-done.56) | copy-start | bytes 6928
  717.5 23.3 %copy-start.59 = (f32[1,512]{1,0:T(1,128)S(1)}, f32[1,512]{1,0:T(1,128)}, u32[]{:S(2)}) copy-start(f32[1,512]{1,0:T(1,128)} %copy-done.58) | copy-start | bytes 6148
  719.0 28.0 %copy-start.22 = (f32[577,512]{1,0:T(8,128)S(1)}, f32[577,512]{1,0:T(8,128)}, u32[]{:S(2)}) copy-start(f32[577,512]{1,0:T(8,128)} %get-tuple-element.281) | copy-start | bytes 3545092
  728.0 19.0 %copy-start.33 = (bf16[577,512]{1,0:T(8,128)(2,1)S(1)}, bf16[577,512]{1,0:T(8,128)(2,1)}, u32[]{:S(2)}) copy-start(bf16[577,512]{1,0:T(8,128)(2,1)} %reduce-scatter.27.cloned.1.call-done) | copy-start | bytes 1772548
  (37 other events, 76.2 us)
Sparse Core Ops, SparseCore 0:
  24.0 11.6 all-gather.31
  37.3 64.6 all-gather.23
  104.1 7.9 all-gather.21
  113.4 31.3 all-gather.25
  153.5 9.7 reduce-scatter.16
  166.7 9.7 reduce-scatter.12
  178.0 10.4 all-gather.39
  190.1 10.4 all-gather.41
  202.1 10.4 all-gather.33
  213.9 141.7 all-gather.29
  368.9 5.5 all-gather.27
  392.6 4.9 reduce-scatter.24
  410.1 4.8 reduce-scatter.20
  417.9 9.0 reduce-scatter.14
  429.2 9.8 reduce-scatter.18
  441.1 10.4 all-gather.35
  453.0 10.4 all-gather.37
  467.5 28.3 reduce-scatter.30
  498.3 75.4 reduce-scatter.34
  575.9 77.2 reduce-scatter.32
  655.6 60.7 reduce-scatter.28
  719.3 8.6 reduce-scatter.26
  730.9 9.8 reduce-scatter.22
  744.4 89.6 all-reduce.15
